TPU v7x, 128 devices: a whole 4x4x4 slice. The times are simulated.
128 devices in a mesh: lat: 8 (over z, core), lon: 16 (over y, x).
Axes of the slice: x: 4, y: 4, z: 4, core: 2. Of those that a mesh axis runs over, the one named last changes fastest.
Arguments:
- tokens: bfloat16 [128, 1024, 512], P('lat', 'lon'), may hold values from -6 to 6
- norm_gain: float32 [512], replicated, may hold values from 0.25 to 1.75
- w_query: bfloat16 [512, 512], replicated, may hold values from -1 to 1
- w_key: bfloat16 [512, 512], replicated, may hold values from -1 to 1
- w_value: bfloat16 [512, 512], replicated, may hold values from -0.25 to 0.25
- w_out: bfloat16 [512, 512], replicated, may hold values from -0.25 to 0.25
- pool_weight: bfloat16 [4, 64], replicated, may hold values from -0.75 to 0.75
- head_scale: float32 [8], replicated, may hold values from 0.5 to 32
- far_ids: int32 [16, 128, 48], P('lat', 'lon'), may hold values from 0 to 2047, as said below
- far_mask: int32 [16, 128, 48], P('lat', 'lon'), may hold values from 0 to 1, as said below
- mlp_gain: float32 [512], replicated, may hold values from 0.25 to 1.75
- w_up: bfloat16 [512, 2048], replicated, may hold values from -0.25 to 0.25
- w_down: bfloat16 [2048, 512], replicated, may hold values from -0.125 to 0.125
Outputs:
- result: bfloat16 [128, 1024, 512], P('lat', 'lon')
Inputs may be any that keep to these rules, and one draw needn't show every extreme that they name: `far_mask`: used slots come first in each block's list; every block uses at least 12 slots. `far_ids`: the tile of 16 x 64 tokens that one device holds is a grid of blocks; among all list slots of one such tile, used or not, the blocks of any one tile are named at most 6 times, and exactly 6 times for some tiles.
All inputs are finite; a program needn't handle non-finite values.
Results may differ from a plain program's by a relative error of at most 0.006.
The roundings to bfloat16 on the way count: a program that leaves them out, or rounds other values in their place, can miss the bound.
Values may be sent and summed in bfloat16 or wider, within the bound.
A program may use at most 128 MiB of HBM per device.

v0:
```python
import math
import jax
import jax.numpy as jnp
from jax import lax
from jax.sharding import PartitionSpec as P

BLK = 8
SUMROWS = 4
FAR = 48
eps = 1e-06


def padded_2(array, sides, width):
    for axis, dim in sides:
        size, length = (lax.axis_size(axis), array.shape[dim])
        up = [(i, (i + 1) % size) for i in range(size)]
        down = [(j, i) for i, j in up]
        last = lax.slice_in_dim(array, length - width, length, axis=dim)
        first = lax.slice_in_dim(array, 0, width, axis=dim)
        before = lax.ppermute(last, axis, up)
        after = lax.ppermute(first, axis, down)
        array = jnp.concatenate([before, array, after], axis=dim)
    return array


def rms_scale(values, scale_gain):
    wide = values.astype(jnp.float32)
    mean_square = jnp.mean(wide * wide, axis=-1, keepdims=True)
    return (wide * lax.rsqrt(mean_square + eps) * scale_gain).astype(jnp.bfloat16)


def project(values, weight):
    flat = values.reshape(-1, values.shape[-1])
    output = jnp.dot(flat, weight, preferred_element_type=jnp.float32).astype(jnp.bfloat16)
    return output.reshape(values.shape[:-1] + (weight.shape[1],))


def to_blocks(grid):
    row_count, col_count, feature = grid.shape
    shaped = grid.reshape(row_count // BLK, BLK, col_count // BLK, BLK, feature)
    return shaped.transpose(0, 2, 1, 3, 4).reshape(
        row_count // BLK, col_count // BLK, BLK * BLK, feature
    )


def local(
    tokens,
    norm_gain,
    w_query,
    w_key,
    w_value,
    w_out,
    pool_weight,
    head_scale,
    far_ids,
    far_mask,
    mlp_gain,
    w_up,
    w_down,
):
    tok_rows, tok_cols, feature = tokens.shape
    blk_rows = tok_rows // BLK
    blk_cols = tok_cols // BLK
    head_count = head_scale.shape[0]
    head_size = feature // head_count
    lat_count = lax.axis_size("lat")
    lon_count = lax.axis_size("lon")
    lat_index = lax.axis_index("lat")
    normed = rms_scale(tokens, norm_gain)
    query = project(normed, w_query)
    w_pair = jnp.concatenate([w_key, w_value], axis=1)
    paired = project(normed, w_pair)
    blocks = to_blocks(normed).reshape(blk_rows * blk_cols, BLK * BLK, feature)
    pooled = jnp.einsum("rt,btd->brd", pool_weight, blocks, preferred_element_type=jnp.float32)
    pooled = pooled.astype(jnp.bfloat16).reshape(blk_rows * blk_cols * SUMROWS, feature)
    padded = padded_2(paired, (("lat", 0), ("lon", 1)), BLK)
    global_cols = blk_cols * lon_count
    global_row = far_ids // global_cols
    global_col = far_ids % global_cols
    owner = global_row // blk_rows * lon_count + global_col // blk_cols
    inner_block = global_row % blk_rows * blk_cols + global_col % blk_cols
    gathered_index = owner * (blk_rows * blk_cols) + inner_block
    listed = gathered_index.reshape(-1)
    sub_rows = jnp.arange(SUMROWS, dtype=jnp.int32)
    listed_rows = (listed[:, None] * SUMROWS + sub_rows[None, :]).reshape(-1)
    summary = project(pooled, w_pair)
    every_pair = lax.all_gather(summary, ("lat", "lon"), axis=0, tiled=True)
    far_pair = jnp.take(every_pair, listed_rows, axis=0)
    far_pair = far_pair.reshape(blk_rows, blk_cols, FAR * SUMROWS, 2 * feature)
    place = jnp.arange(tok_rows + 2 * BLK, dtype=jnp.int32) + lat_index * tok_rows - BLK
    row_valid = (place >= 0) & (place < tok_rows * lat_count)
    query_blocks = to_blocks(query)
    score_scale = head_scale * (1.0 / math.sqrt(head_size))
    near_width = 3 * BLK * BLK

    def one_row(row_index):
        strip = lax.dynamic_slice_in_dim(padded, row_index * BLK, 3 * BLK, 0)
        shaped = strip.reshape(3 * BLK, blk_cols + 2, BLK, 2, head_count, head_size)
        key_grid = shaped[:, :, :, 0]
        value_grid = shaped[:, :, :, 1]
        row_query = lax.dynamic_index_in_dim(query_blocks, row_index, 0, keepdims=False)
        query_heads = row_query.reshape(blk_cols, BLK * BLK, head_count, head_size)
        far_rows = lax.dynamic_index_in_dim(far_pair, row_index, 0, keepdims=False)
        far_heads = far_rows.reshape(blk_cols, FAR * SUMROWS, 2, head_count, head_size)
        scores = []
        for offset in range(3):
            part_score = jnp.einsum(
                "cqhd,rckhd->chqrk",
                query_heads,
                key_grid[:, offset : offset + blk_cols],
                preferred_element_type=jnp.float32,
            )
            scores.append(part_score.reshape(blk_cols, head_count, BLK * BLK, near_width))
        scores.append(
            jnp.einsum(
                "cqhd,ckhd->chqk",
                query_heads,
                far_heads[:, :, 0],
                preferred_element_type=jnp.float32,
            )
        )
        score = jnp.concatenate(scores, axis=-1) * score_scale[None, :, None, None]
        strip_valid = lax.dynamic_slice_in_dim(row_valid, row_index * BLK, 3 * BLK, 0)
        near_valid = jnp.broadcast_to(strip_valid[:, None], (3 * BLK, BLK)).reshape(-1)
        row_mask = lax.dynamic_index_in_dim(far_mask, row_index, 0, keepdims=False)
        far_valid = jnp.repeat(row_mask > 0, SUMROWS, axis=1)
        near_all = jnp.concatenate([near_valid, near_valid, near_valid])
        valid = jnp.concatenate(
            [jnp.broadcast_to(near_all[None, :], (blk_cols, near_all.shape[0])), far_valid], axis=1
        )
        keep = valid[:, None, None, :]
        highest = jnp.max(jnp.where(keep, score, -1e30), axis=-1, keepdims=True)
        expo = jnp.exp(jnp.where(keep, score - highest, -1e30))
        weights = (expo / jnp.sum(expo, axis=-1, keepdims=True)).astype(jnp.bfloat16)
        mixed = jnp.einsum(
            "chqk,ckhd->cqhd",
            weights[..., 3 * near_width :],
            far_heads[:, :, 1],
            preferred_element_type=jnp.float32,
        )
        for offset in range(3):
            part_weight = weights[..., offset * near_width : (offset + 1) * near_width].reshape(
                blk_cols, head_count, BLK * BLK, 3 * BLK, BLK
            )
            mixed = mixed + jnp.einsum(
                "chqrk,rckhd->cqhd",
                part_weight,
                value_grid[:, offset : offset + blk_cols],
                preferred_element_type=jnp.float32,
            )
        return mixed.astype(jnp.bfloat16).reshape(blk_cols, BLK * BLK, feature)

    attended = lax.map(one_row, jnp.arange(blk_rows, dtype=jnp.int32))
    attn = (
        attended.reshape(blk_rows, blk_cols, BLK, BLK, feature)
        .transpose(0, 2, 1, 3, 4)
        .reshape(tok_rows * tok_cols, feature)
    )
    mixed = (
        tokens.reshape(-1, feature).astype(jnp.float32)
        + jnp.dot(attn, w_out, preferred_element_type=jnp.float32)
    ).astype(jnp.bfloat16)
    normed_two = rms_scale(mixed, mlp_gain)
    hidden = jax.nn.gelu(
        jnp.dot(normed_two, w_up, preferred_element_type=jnp.float32), approximate=True
    ).astype(jnp.bfloat16)
    result = (
        mixed.astype(jnp.float32) + jnp.dot(hidden, w_down, preferred_element_type=jnp.float32)
    ).astype(jnp.bfloat16)
    return result.reshape(tok_rows, tok_cols, feature)


def solution(mesh):
    return jax.shard_map(
        local,
        mesh=mesh,
        in_specs=(
            P("lat", "lon", None),
            P(),
            P(),
            P(),
            P(),
            P(),
            P(),
            P(),
            P("lat", "lon", None),
            P("lat", "lon", None),
            P(),
            P(),
            P(),
        ),
        out_specs=P("lat", "lon", None),
        check_vma=False,
    )
```

profile of v0, /device:TPU:1, one launch (start us, length us, event | category | flops | bytes accessed | tf_op | source)
XLA Modules:
  0.0 528.9 jit_solution(14609142763297510466)
XLA Ops:
  31.4 6.1 %collective-permute-done = bf16[8,64,1024]{2,1,0:T(8,128)(2,1)S(1)} collective-permute-done((bf16[8,64,1024]{2,1,0:T(8,128)(2,1)}, bf16[8,64,1024]{2,1,0:T(8,128)(2,1)S(1)}, u32[]{:S(2)}, u32[]{:S(2)}) %collective-permute-start) | collective-permute-done | bytes 1048608 | tf_op jit(solution)/shard_map/ppermute | solution.py:20
  42.7 3.8 collective-permute-start.3
  46.6 13.8 %collective-permute-done.2 = bf16[32,8,1024]{2,1,0:T(8,128)(2,1)S(1)} collective-permute-done((bf16[32,8,1024]{2,1,0:T(8,128)(2,1)S(1)}, bf16[32,8,1024]{2,1,0:T(8,128)(2,1)S(1)}, u32[]{:S(2)}, u32[]{:S(2)}) %collective-permute-start.2) | collective-permute-done | bytes 524320 | tf_op jit(solution)/shard_map/ppermute | solution.py:20
  60.4 5.4 %pad_maximum_fusion = bf16[32,80,1024]{2,1,0:T(8,128)(2,1)} fusion(bf16[32,8,1024]{2,1,0:T(8,128)(2,1)S(1)} %collective-permute-done.3, bf16[8,64,1024]{2,1,0:T(8,128)(2,1)} %collective-permute-done.1, bf16[16,64,1024]{2,1,0:T(8,128)(2,1)S(1)} %bitcast.161, bf16[8,64,1024]{2,1,0:T(8,128)(2,1)S(1)} %collective-permute-done, ...), kind=kLoop, calls=%fused_computation.59 | loop fusion | flops 26214400 | bytes 10485760 | tf_op jit(solution)/shard_map/concatenate | solution.py:22
  65.8 38.2 %all-gather.2.cloned.1.call-done = bf16[8192,1024]{1,0:T(8,128)(2,1)} async-done(((bf16[64,1024]{1,0:T(8,128)(2,1)}), bf16[8192,1024]{1,0:T(8,128)(2,1)}) %all-gather.2.cloned.1.call-update) | async-done | bytes 16777232 | tf_op jit(solution)/shard_map/all_gather | solution.py:87
  104.0 23.9 %gather_fusion = bf16[3072,1024]{1,0:T(8,128)(2,1)} fusion(bf16[8192,1024]{1,0:T(8,128)(2,1)} %all-gather.2.cloned.1.call-done, s32[3072]{0:T(1024)S(1)} %broadcast_clamp_fusion), kind=kCustom, calls=%fused_computation | custom fusion | bytes 12595200 | tf_op jit(solution)/shard_map/jit(_take)/gather | solution.py:88
  128.0 11.1 %copy.73 = bf16[2,8,192,1024]{2,3,1,0:T(8,128)(2,1)} copy(bf16[2,8,192,1024]{3,2,1,0:T(8,128)(2,1)} %bitcast.159) | data formatting | bytes 12582912 | tf_op jit(solution)/shard_map/jit(_take)/gather | solution.py:88
  139.0 7.6 %broadcast_select_fusion = bf16[2,8,192,1024]{2,3,1,0:T(8,128)(2,1)} fusion(bf16[2,8,192,1024]{2,3,1,0:T(8,128)(2,1)} %copy.73, pred[2,8,192]{2,1,0:T(8,128)(4,1)S(1)} %compare_and_fusion), kind=kLoop, calls=%fused_computation.58 | loop fusion | flops 3145728 | bytes 12585984 | tf_op jit(solution)/shard_map/jit(_take)/select_n | solution.py:88
  146.6 364.2 %while.10 = (s32[]{:T(128)}, bf16[2,8,64,512]{3,2,1,0:T(8,128)(2,1)}, s32[2]{0:T(128)S(1)}, bf16[2,8,192,1024]{2,3,1,0:T(8,128)(2,1)}, pred[32]{0:T(512)(128)(4,...) while((s32[]{:T(128)}, ...), condition=%wide.region_4.5_spmd, body=%wide.region_1.4_spmd.sunk | while | flops 850403584 | bytes 223804016 | solution.py:153
  147.7 4.6 constant_dynamic-slice_fusion.11
  152.4 11.2 %reshape.180 = bf16[24,10,8,2,8,64]{5,4,3,2,1,0:T(8,128)(2,1)} reshape(bf16[24,80,1024]{2,1,0:T(8,128)(2,1)} %constant_dynamic-slice_fusion.11) | data formatting | bytes 7864320 | tf_op jit(solution)/shard_map/while/body/eval_jaxpr/reshape | solution.py:98
  163.6 5.6 %fusion.127 = (bf16[24,10,8,1,8,64]{5,4,3,2,1,0:T(8,128)(2,1)}, bf16[24,10,8,1,8,64]{5,4,3,2,1,0:T(8,128)(2,1)S(1)}) fusion(bf16[24,10,8,2,8,64]{5,4,3,2,1,0:T(8,128)(2,1)} %reshape.180), kind=kLoop, calls=%fused_computation.135.clone.1 | loop fusion | bytes 7864320 | tf_op jit(solution)/shard_map/while/body/eval_jaxpr/slice | solution.py:100
  169.2 4.9 copy.160
  183.0 4.0 copy.161
  187.0 6.8 %copy.162 = f32[8,8,64,192]{3,2,1,0:T(8,128)} copy(f32[8,8,64,192]{2,3,1,0:T(8,128)} %bitcast.150) | data formatting | bytes 6291456 | tf_op jit(solution)/shard_map/while/body/eval_jaxpr/reshape | solution.py:113
  197.5 4.1 copy.163
  201.6 6.3 %copy.164 = f32[8,8,64,192]{3,2,1,0:T(8,128)} copy(f32[8,8,64,192]{2,3,1,0:T(8,128)} %bitcast.151) | data formatting | bytes 6291456 | tf_op jit(solution)/shard_map/while/body/eval_jaxpr/reshape | solution.py:113
  211.6 3.9 copy.165
  215.5 6.3 %copy.166 = f32[8,8,64,192]{3,2,1,0:T(8,128)} copy(f32[8,8,64,192]{2,3,1,0:T(8,128)} %bitcast.152) | data formatting | bytes 6291456 | tf_op jit(solution)/shard_map/while/body/eval_jaxpr/reshape | solution.py:113
  227.0 41.4 %fusion.131 = (f32[8,8,64]{2,1,0:T(8,128)S(1)}, f32[8,8,64,768]{3,2,1,0:T(8,128)}) fusion(pred[8,768]{1,0:T(8,128)(4,1)S(1)} %pad_add_fusion.5, f32[8]{0:T(128)S(1)} %get-tuple-element.209, f32[8,8,64,192]{3,2,1,0:T(8,128)S(1)} %fusion.126, f32[8,8,64,192]{3,2,1,0:T(8,128)} %copy.162, f32[8,8,64,192]{3,2,1,0:T(8,128)} %copy.164, ...), kind=kOutput, calls=%fused_computation.137.clone.1 | output fusion | flops 37749504 | bytes 25188384 | tf_op jit(solution)/shard_map/while/body/eval_jaxpr/sub | solution.py:133
  268.4 8.0 %divide_convert_fusion.2 = bf16[8,8,64,768]{3,2,1,0:T(8,128)(2,1)} fusion(f32[8,8,64,768]{3,2,1,0:T(8,128)} %get-tuple-element.165, f32[8,8,64]{2,1,0:T(8,128)S(1)} %get-tuple-element.166), kind=kLoop, calls=%fused_computation.3.clone.1 | loop fusion | flops 6291456 | bytes 18890752 | tf_op jit(solution)/shard_map/while/body/eval_jaxpr/convert_element_type | solution.py:134
  276.5 7.2 %fusion.132 = (bf16[8,8,64,192]{3,2,1,0:T(8,128)(2,1)}, bf16[8,8,64,192]{3,2,1,0:T(8,128)(2,1)}, bf16[8,8,64,192]{3,2,1,0:T(8,128)(2,1)}) fusion(bf16[8,8,64,768]{3,2,1,0:T(8,128)(2,1)} %divide_convert_fusion.2), kind=kLoop, calls=%fused_computation.136.clone.1 | loop fusion | bytes 9437184 | tf_op jit(solution)/shard_map/while/body/eval_jaxpr/slice | solution.py:142
  283.7 4.5 copy.169
  288.1 8.2 %fusion.135 = f32[8,8,64,64,1]{3,2,4,1,0:T(8,128)} fusion(bf16[8,8,64,24,8]{2,4,3,1,0:T(8,128)(2,1)} %bitcast.156, bf16[24,10,8,1,8,64]{5,4,3,2,1,0:T(8,128)(2,1)} %get-tuple-element.168), kind=kOutput, calls=%fused_computation.24.clone.1 | convolution fusion | flops 100663296 | bytes 4587520 | tf_op jit(solution)/shard_map/while/body/eval_jaxpr/chqrk,rckhd->cqhd/dot_general | solution.py:145
  296.3 4.7 copy.168
  301.0 8.2 %fusion.134 = f32[8,8,64,64,1]{3,2,4,1,0:T(8,128)} fusion(bf16[8,8,64,24,8]{2,4,3,1,0:T(8,128)(2,1)} %bitcast.158, bf16[24,10,8,1,8,64]{5,4,3,2,1,0:T(8,128)(2,1)} %get-tuple-element.168), kind=kOutput, calls=%fused_computation.22.clone.1 | convolution fusion | flops 100663296 | bytes 4587520 | tf_op jit(solution)/shard_map/while/body/eval_jaxpr/chqrk,rckhd->cqhd/dot_general | solution.py:145
  309.2 4.5 copy.167
  313.7 7.0 %fusion.133 = f32[8,8,64,64,1]{3,2,4,1,0:T(8,128)S(1)} fusion(bf16[8,8,64,24,8]{2,4,3,1,0:T(8,128)(2,1)} %bitcast.157, bf16[24,10,8,1,8,64]{5,4,3,2,1,0:T(8,128)(2,1)} %get-tuple-element.168), kind=kOutput, calls=%fused_computation.20.clone.1 | convolution fusion | flops 100663296 | bytes 4587520 | tf_op jit(solution)/shard_map/while/body/eval_jaxpr/chqrk,rckhd->cqhd/dot_general | solution.py:145
  328.0 4.6 constant_dynamic-slice_fusion.11
  332.6 11.2 %reshape.180 = bf16[24,10,8,2,8,64]{5,4,3,2,1,0:T(8,128)(2,1)} reshape(bf16[24,80,1024]{2,1,0:T(8,128)(2,1)} %constant_dynamic-slice_fusion.11) | data formatting | bytes 7864320 | tf_op jit(solution)/shard_map/while/body/eval_jaxpr/reshape | solution.py:98
  343.8 5.6 %fusion.127 = (bf16[24,10,8,1,8,64]{5,4,3,2,1,0:T(8,128)(2,1)}, bf16[24,10,8,1,8,64]{5,4,3,2,1,0:T(8,128)(2,1)S(1)}) fusion(bf16[24,10,8,2,8,64]{5,4,3,2,1,0:T(8,128)(2,1)} %reshape.180), kind=kLoop, calls=%fused_computation.135.clone.1 | loop fusion | bytes 7864320 | tf_op jit(solution)/shard_map/while/body/eval_jaxpr/slice | solution.py:100
  349.5 4.9 copy.160
  363.3 4.0 copy.161
  367.3 6.5 %copy.162 = f32[8,8,64,192]{3,2,1,0:T(8,128)} copy(f32[8,8,64,192]{2,3,1,0:T(8,128)} %bitcast.150) | data formatting | bytes 6291456 | tf_op jit(solution)/shard_map/while/body/eval_jaxpr/reshape | solution.py:113
  377.4 4.1 copy.163
  381.5 6.3 %copy.164 = f32[8,8,64,192]{3,2,1,0:T(8,128)} copy(f32[8,8,64,192]{2,3,1,0:T(8,128)} %bitcast.151) | data formatting | bytes 6291456 | tf_op jit(solution)/shard_map/while/body/eval_jaxpr/reshape | solution.py:113
  391.5 3.9 copy.165
  395.5 6.3 %copy.166 = f32[8,8,64,192]{3,2,1,0:T(8,128)} copy(f32[8,8,64,192]{2,3,1,0:T(8,128)} %bitcast.152) | data formatting | bytes 6291456 | tf_op jit(solution)/shard_map/while/body/eval_jaxpr/reshape | solution.py:113
  407.0 41.5 %fusion.131 = (f32[8,8,64]{2,1,0:T(8,128)S(1)}, f32[8,8,64,768]{3,2,1,0:T(8,128)}) fusion(pred[8,768]{1,0:T(8,128)(4,1)S(1)} %pad_add_fusion.5, f32[8]{0:T(128)S(1)} %get-tuple-element.209, f32[8,8,64,192]{3,2,1,0:T(8,128)S(1)} %fusion.126, f32[8,8,64,192]{3,2,1,0:T(8,128)} %copy.162, f32[8,8,64,192]{3,2,1,0:T(8,128)} %copy.164, ...), kind=kOutput, calls=%fused_computation.137.clone.1 | output fusion | flops 37749504 | bytes 25188384 | tf_op jit(solution)/shard_map/while/body/eval_jaxpr/sub | solution.py:133
  448.4 8.0 %divide_convert_fusion.2 = bf16[8,8,64,768]{3,2,1,0:T(8,128)(2,1)} fusion(f32[8,8,64,768]{3,2,1,0:T(8,128)} %get-tuple-element.165, f32[8,8,64]{2,1,0:T(8,128)S(1)} %get-tuple-element.166), kind=kLoop, calls=%fused_computation.3.clone.1 | loop fusion | flops 6291456 | bytes 18890752 | tf_op jit(solution)/shard_map/while/body/eval_jaxpr/convert_element_type | solution.py:134
  456.5 7.2 %fusion.132 = (bf16[8,8,64,192]{3,2,1,0:T(8,128)(2,1)}, bf16[8,8,64,192]{3,2,1,0:T(8,128)(2,1)}, bf16[8,8,64,192]{3,2,1,0:T(8,128)(2,1)}) fusion(bf16[8,8,64,768]{3,2,1,0:T(8,128)(2,1)} %divide_convert_fusion.2), kind=kLoop, calls=%fused_computation.136.clone.1 | loop fusion | bytes 9437184 | tf_op jit(solution)/shard_map/while/body/eval_jaxpr/slice | solution.py:142
  463.6 4.5 copy.169
  468.1 8.2 %fusion.135 = f32[8,8,64,64,1]{3,2,4,1,0:T(8,128)} fusion(bf16[8,8,64,24,8]{2,4,3,1,0:T(8,128)(2,1)} %bitcast.156, bf16[24,10,8,1,8,64]{5,4,3,2,1,0:T(8,128)(2,1)} %get-tuple-element.168), kind=kOutput, calls=%fused_computation.24.clone.1 | convolution fusion | flops 100663296 | bytes 4587520 | tf_op jit(solution)/shard_map/while/body/eval_jaxpr/chqrk,rckhd->cqhd/dot_general | solution.py:145
  476.3 4.9 copy.168
  481.2 8.2 %fusion.134 = f32[8,8,64,64,1]{3,2,4,1,0:T(8,128)} fusion(bf16[8,8,64,24,8]{2,4,3,1,0:T(8,128)(2,1)} %bitcast.158, bf16[24,10,8,1,8,64]{5,4,3,2,1,0:T(8,128)(2,1)} %get-tuple-element.168), kind=kOutput, calls=%fused_computation.22.clone.1 | convolution fusion | flops 100663296 | bytes 4587520 | tf_op jit(solution)/shard_map/while/body/eval_jaxpr/chqrk,rckhd->cqhd/dot_general | solution.py:145
  489.4 4.5 copy.167
  493.9 7.0 %fusion.133 = f32[8,8,64,64,1]{3,2,4,1,0:T(8,128)S(1)} fusion(bf16[8,8,64,24,8]{2,4,3,1,0:T(8,128)(2,1)} %bitcast.157, bf16[24,10,8,1,8,64]{5,4,3,2,1,0:T(8,128)(2,1)} %get-tuple-element.168), kind=kOutput, calls=%fused_computation.20.clone.1 | convolution fusion | flops 100663296 | bytes 4587520 | tf_op jit(solution)/shard_map/while/body/eval_jaxpr/chqrk,rckhd->cqhd/dot_general | solution.py:145
  514.4 7.4 %fusion.43 = bf16[1024,512]{1,0:T(8,128)(2,1)} fusion(bf16[1024,512]{1,0:T(8,128)(2,1)S(1)} %get-tuple-element.101, bf16[2048,512]{1,0:T(8,128)(2,1)S(1)} %copy-done, bf16[512,2048]{1,0:T(8,128)(2,1)} %param.26, f32[512]{0:T(512)S(1)} %copy-done.13, f32[1024]{0:T(1024)S(1)} %add_rsqrt_fusion.1), kind=kOutput, calls=%fused_computation.67 | convolution fusion | flops 4317511680 | bytes 6297600 | tf_op jit(solution)/shard_map/dot_general | solution.py:168
  (122 shorter events, 85.6 us)
Async XLA Ops:
  6.5 507.8 %copy-start = (bf16[2048,512]{1,0:T(8,128)(2,1)S(1)}, bf16[2048,512]{1,0:T(8,128)(2,1)}, u32[]{:S(2)}) copy-start(bf16[2048,512]{1,0:T(8,128)(2,1)} %param.27) | copy-start | bytes 6291460
  6.5 5.2 copy-start.12
  6.5 97.5 %all-gather.2.cloned.1.call-start = ((), (), s32[]{:S(2)}) async-start(), calls=%async_computation | async-start | bytes 16908288 | tf_op jit(solution)/shard_map/all_gather | solution.py:87
  11.6 7.0 %copy-start.7 = (bf16[16,64,512]{2,1,0:T(8,128)(2,1)}, bf16[16,64,512]{2,1,0:T(8,128)(2,1)S(1)}, u32[]{:S(2)}) copy-start(bf16[16,64,512]{2,1,0:T(8,128)(2,1)S(1)} %multiply_convert_fusion) | copy-start | bytes 3145732
  18.6 1.3 copy-start.5
  19.9 4.6 copy-start.11
  21.5 16.0 %collective-permute-start = (bf16[8,64,1024]{2,1,0:T(8,128)(2,1)}, bf16[8,64,1024]{2,1,0:T(8,128)(2,1)S(1)}, u32[]{:S(2)}, u32[]{:S(2)}) collective-permute-start(bf16[8,64,1024]{2,1,0:T(8,128)(2,1)} %bitcast.38), channel_id=1, source_target_pairs={{0,16},{16,32},{32,48},{48,64},{64,80},{80,96},{96,112},{112,0},{1... | collective-permute-start | bytes 3145736 | tf_op jit(solution)/shard_map/ppermute | solution.py:20
  24.5 15.8 %collective-permute-start.1 = (bf16[8,64,1024]{2,1,0:T(8,128)(2,1)}, bf16[8,64,1024]{2,1,0:T(8,128)(2,1)}, u32[]{:S(2)}, u32[]{:S(2)}) collective-permute-start(bf16[8,64,1024]{2,1,0:T(8,128)(2,1)} %bitcast.40), channel_id=1, source_target_pairs={{16,0},{32,16},{48,32},{64,48},{80,64},{96,80},{112,96},{0,112},{1... | collective-permute-start | bytes 3145736 | tf_op jit(solution)/shard_map/ppermute | solution.py:21
  28.1 3.2 copy-start.14
  28.1 3.2 copy-start.10
  30.2 16.3 %copy-start.8 = (s32[2,8,192]{2,1,0:T(8,128)S(1)}, s32[2,8,192]{2,1,0:T(8,128)}, u32[]{:S(2)}) copy-start(s32[2,8,192]{2,1,0:T(8,128)} %copy.71) | copy-start | bytes 36868
  31.3 29.1 %copy-start.6 = (bf16[1024,1024]{1,0:T(8,128)(2,1)S(1)}, bf16[1024,1024]{1,0:T(8,128)(2,1)}, u32[]{:S(2)}) copy-start(bf16[1024,1024]{1,0:T(8,128)(2,1)} %copy-done.5) | copy-start | bytes 6291460
  41.5 18.9 %collective-permute-start.2 = (bf16[32,8,1024]{2,1,0:T(8,128)(2,1)S(1)}, bf16[32,8,1024]{2,1,0:T(8,128)(2,1)S(1)}, u32[]{:S(2)}, u32[]{:S(2)}) collective-permute-start(bf16[32,8,1024]{2,1,0:T(8,128)(2,1)S(1)} %get-tuple-element.96), channel_id=1, source_target_pairs={{0,1},{1,2},{2,3},{3,4},{4,5},{5,6},{6,7},{7,8},{8,9},{9,10},{10,1... | collective-permute-start | bytes 1572872 | tf_op jit(solution)/shard_map/ppermute | solution.py:20
  42.7 17.6 %collective-permute-start.3 = (bf16[32,8,1024]{2,1,0:T(8,128)(2,1)S(1)}, bf16[32,8,1024]{2,1,0:T(8,128)(2,1)S(1)}, u32[]{:S(2)}, u32[]{:S(2)}) collective-permute-start(bf16[32,8,1024]{2,1,0:T(8,128)(2,1)S(1)} %get-tuple-element.97), channel_id=1, source_target_pairs={{1,0},{2,1},{3,2},{4,3},{5,4},{6,5},{7,6},{8,7},{9,8},{10,9},{11,1... | collective-permute-start | bytes 1572872 | tf_op jit(solution)/shard_map/ppermute | solution.py:21
  139.0 7.6 %copy-start.9 = (s32[2,8,48]{2,1,0:T(8,128)S(1)}, s32[2,8,48]{2,1,0:T(8,128)}, u32[]{:S(2)}) copy-start(s32[2,8,48]{2,1,0:T(8,128)} %param.24) | copy-start | bytes 9220
  225.0 2.0 copy-start.1
  313.7 7.0 %copy-start.2 = (bf16[1,8,192,1024]{2,3,1,0:T(8,128)(2,1)S(1)}, bf16[1,8,192,1024]{2,3,1,0:T(8,128)(2,1)}, u32[]{:S(2)}) copy-start(bf16[1,8,192,1024]{2,3,1,0:T(8,128)(2,1)} %copy-done.1) | copy-start | bytes 9437188 | tf_op jit(solution)/shard_map/while
  313.7 7.0 %copy-start.3 = (f32[8,8,64,64,1]{3,2,4,1,0:T(8,128)S(1)}, f32[8,8,64,64,1]{3,2,4,1,0:T(8,128)}, u32[]{:S(2)}) copy-start(f32[8,8,64,64,1]{3,2,4,1,0:T(8,128)} %fusion.135) | copy-start | bytes 3145732 | tf_op jit(solution)/shard_map/while
  313.7 7.0 %copy-start.4 = (f32[8,8,64,64,1]{3,2,4,1,0:T(8,128)S(1)}, f32[8,8,64,64,1]{3,2,4,1,0:T(8,128)}, u32[]{:S(2)}) copy-start(f32[8,8,64,64,1]{3,2,4,1,0:T(8,128)} %fusion.134) | copy-start | bytes 3145732 | tf_op jit(solution)/shard_map/while
  404.9 2.0 copy-start.1
  493.9 7.0 %copy-start.2 = (bf16[1,8,192,1024]{2,3,1,0:T(8,128)(2,1)S(1)}, bf16[1,8,192,1024]{2,3,1,0:T(8,128)(2,1)}, u32[]{:S(2)}) copy-start(bf16[1,8,192,1024]{2,3,1,0:T(8,128)(2,1)} %copy-done.1) | copy-start | bytes 9437188 | tf_op jit(solution)/shard_map/while
  493.9 7.0 %copy-start.3 = (f32[8,8,64,64,1]{3,2,4,1,0:T(8,128)S(1)}, f32[8,8,64,64,1]{3,2,4,1,0:T(8,128)}, u32[]{:S(2)}) copy-start(f32[8,8,64,64,1]{3,2,4,1,0:T(8,128)} %fusion.135) | copy-start | bytes 3145732 | tf_op jit(solution)/shard_map/while
  493.9 7.0 %copy-start.4 = (f32[8,8,64,64,1]{3,2,4,1,0:T(8,128)S(1)}, f32[8,8,64,64,1]{3,2,4,1,0:T(8,128)}, u32[]{:S(2)}) copy-start(f32[8,8,64,64,1]{3,2,4,1,0:T(8,128)} %fusion.134) | copy-start | bytes 3145732 | tf_op jit(solution)/shard_map/while
  510.8 3.6 copy-start.13
Sparse Core Ops, SparseCore 0:
  16.2 87.7 all-gather.1
where the time goes:
time: 539 us; the launch traced here: 529 us
  local copies, waits for them, and re-layouts  227 us (42%)
  other arithmetic  117 us (22%)
  matrix products  92.3 us (17%)
  waiting for transfers between devices  60.9 us (11%)
  between operations  13.8 us (3%)
  loops' own time  9.32 us (2%)
  starting transfers between devices  8.05 us (1%)
    sub x2, other arithmetic, one_row(): expo = jnp.exp(jnp.where(keep, score - highest, -1e+30))  82.9 us
    dot_general x6, matrix products, one_row(): jnp.einsum('chqrk,rckhd->cqhd', part_weight, value_grid[:, offset:offset...  46.7 us
    slice x8, local copies, waits for them, and re-layouts, one_row(): weights[..., offset * near_width:(offset + 1) * near_width]  41.8 us
    reshape x6, local copies, waits for them, and re-layouts, one_row(): part_score.reshape(blk_cols, head_count, BLK * BLK, near_width)  38.6 us
    all_gather x1, waiting for transfers between devices, local(): every_pair = lax.all_gather(summary, ('lat', 'lon'), axis=0, tiled=True)  38.2 us
    gather x2, local copies, waits for them, and re-layouts, local(): far_pair = jnp.take(every_pair, listed_rows, axis=0)  35 us
    dot_general x6, local copies, waits for them, and re-layouts, one_row(): jnp.einsum('cqhd,rckhd->chqrk', query_heads, key_grid[:, offset:offset +...  24 us
    reshape x2, local copies, waits for them, and re-layouts, one_row(): shaped = strip.reshape(3 * BLK, blk_cols + 2, BLK, 2, head_count, head_size)  22.4 us
  transfers between devices with their start and end apart: 5, of which 4 were waited for; matrix products, arithmetic and copies ran while one was open for 3% of the time, Pallas kernels for 0%

commit v1 on v0

--- a/solution.py
+++ b/solution.py
@@ -84,7 +84,12 @@
     sub_rows = jnp.arange(SUMROWS, dtype=jnp.int32)
     listed_rows = (listed[:, None] * SUMROWS + sub_rows[None, :]).reshape(-1)
     summary = project(pooled, w_pair)
-    every_pair = lax.all_gather(summary, ("lat", "lon"), axis=0, tiled=True)
+    every_pair = jnp.concatenate(
+        lax.all_to_all(
+            jnp.stack(lax.axis_size(("lat", "lon")) * [summary], axis=0), ("lat", "lon"), 0, 0
+        ),
+        axis=0,
+    )
     far_pair = jnp.take(every_pair, listed_rows, axis=0)
     far_pair = far_pair.reshape(blk_rows, blk_cols, FAR * SUMROWS, 2 * feature)
     place = jnp.arange(tok_rows + 2 * BLK, dtype=jnp.int32) + lat_index * tok_rows - BLK

time: 539 us -> 723 us (1.34)
  the two profiles are of different devices: /device:TPU:1 before, /device:TPU:12 now
where the time goes in v1:
time: 723 us; the launch traced here: 713 us
  local copies, waits for them, and re-layouts  234 us (32%)
  waiting for transfers between devices  234 us (32%)
  other arithmetic  117 us (16%)
  matrix products  91.7 us (13%)
  starting transfers between devices  25.7 us (4%)
  loops' own time  10.3 us (1%)
    ppermute x2, waiting for transfers between devices, padded_2(): before = lax.ppermute(last, axis, up)  201 us
    sub x2, other arithmetic, one_row(): expo = jnp.exp(jnp.where(keep, score - highest, -1e+30))  82.9 us
    dot_general x6, matrix products, one_row(): jnp.einsum('chqrk,rckhd->cqhd', part_weight, value_grid[:, offset:offset...  46.8 us
    slice x8, local copies, waits for them, and re-layouts, one_row(): weights[..., offset * near_width:(offset + 1) * near_width]  42.2 us
    reshape x6, local copies, waits for them, and re-layouts, one_row(): part_score.reshape(blk_cols, head_count, BLK * BLK, near_width)  38.6 us
    gather x2, local copies, waits for them, and re-layouts, local(): far_pair = jnp.take(every_pair, listed_rows, axis=0)  34.9 us
    ppermute x2, waiting for transfers between devices, padded_2(): after = lax.ppermute(first, axis, down)  32.5 us
    dot_general x6, local copies, waits for them, and re-layouts, one_row(): jnp.einsum('cqhd,rckhd->chqrk', query_heads, key_grid[:, offset:offset +...  23.9 us
  transfers between devices with their start and end apart: 5, of which 3 were waited for; matrix products, arithmetic and copies ran while one was open for 2% of the time, Pallas kernels for 0%

profile of v1, /device:TPU:12, one launch (start us, length us, event | category | flops | bytes accessed | tf_op | source)
XLA Modules:
  0.0 713.0 jit_solution(5621016355881696295)
XLA Ops:
  8.9 6.2 stack.2
  15.1 10.8 %all-to-all-start = ((bf16[128,64,1024]{2,1,0:T(8,128)(2,1)}), bf16[128,64,1024]{2,1,0:T(8,128)(2,1)}, u32[]{:S(2)}, u32[]{:S(2)}) async-start(bf16[128,64,1024]{2,1,0:T(8,128)(2,1)} %stack.2), calls=%async_computation | async-start | bytes 33554432 | tf_op jit(solution)/shard_map/all_to_all | solution.py:88
  41.4 117.5 %collective-permute-done = bf16[8,64,1024]{2,1,0:T(8,128)(2,1)S(1)} collective-permute-done((bf16[8,64,1024]{2,1,0:T(8,128)(2,1)}, bf16[8,64,1024]{2,1,0:T(8,128)(2,1)S(1)}, u32[]{:S(2)}, u32[]{:S(2)}) %collective-permute-start) | collective-permute-done | bytes 1048608 | tf_op jit(solution)/shard_map/ppermute | solution.py:20
  160.1 11.6 %collective-permute-start.2 = (bf16[32,8,1024]{2,1,0:T(8,128)(2,1)S(1)}, bf16[32,8,1024]{2,1,0:T(8,128)(2,1)S(1)}, u32[]{:S(2)}, u32[]{:S(2)}) collective-permute-start(bf16[32,8,1024]{2,1,0:T(8,128)(2,1)S(1)} %get-tuple-element.96), channel_id=1, source_target_pairs={{0,1},{1,2},{2,3},{3,4},{4,5},{5,6},{6,7},{7,8},{8,9},{9,10},{10,1... | collective-permute-start | bytes 1572872 | tf_op jit(solution)/shard_map/ppermute | solution.py:20
  171.8 83.8 %collective-permute-done.2 = bf16[32,8,1024]{2,1,0:T(8,128)(2,1)S(1)} collective-permute-done((bf16[32,8,1024]{2,1,0:T(8,128)(2,1)S(1)}, bf16[32,8,1024]{2,1,0:T(8,128)(2,1)S(1)}, u32[]{:S(2)}, u32[]{:S(2)}) %collective-permute-start.2) | collective-permute-done | bytes 524320 | tf_op jit(solution)/shard_map/ppermute | solution.py:20
  255.6 32.5 %collective-permute-done.3 = bf16[32,8,1024]{2,1,0:T(8,128)(2,1)S(1)} collective-permute-done((bf16[32,8,1024]{2,1,0:T(8,128)(2,1)S(1)}, bf16[32,8,1024]{2,1,0:T(8,128)(2,1)S(1)}, u32[]{:S(2)}, u32[]{:S(2)}) %collective-permute-start.3) | collective-permute-done | bytes 524320 | tf_op jit(solution)/shard_map/ppermute | solution.py:21
  288.1 5.4 pad_maximum_fusion
  293.5 23.9 %gather_fusion = bf16[3072,1024]{1,0:T(8,128)(2,1)} fusion(bf16[8192,1024]{1,0:T(8,128)(2,1)} %bitcast.32, s32[3072]{0:T(1024)S(1)} %broadcast_clamp_fusion), kind=kCustom, calls=%fused_computation | custom fusion | bytes 12595200 | tf_op jit(solution)/shard_map/jit(_take)/gather | solution.py:93
  317.4 11.0 %copy.73 = bf16[2,8,192,1024]{2,3,1,0:T(8,128)(2,1)} copy(bf16[2,8,192,1024]{3,2,1,0:T(8,128)(2,1)} %bitcast.160) | data formatting | bytes 12582912 | tf_op jit(solution)/shard_map/jit(_take)/gather | solution.py:93
  328.4 7.5 %broadcast_select_fusion = bf16[2,8,192,1024]{2,3,1,0:T(8,128)(2,1)} fusion(bf16[2,8,192,1024]{2,3,1,0:T(8,128)(2,1)} %copy.73, pred[2,8,192]{2,1,0:T(8,128)(4,1)S(1)} %compare_and_fusion), kind=kLoop, calls=%fused_computation.58 | loop fusion | flops 3145728 | bytes 12585984 | tf_op jit(solution)/shard_map/jit(_take)/select_n | solution.py:93
  336.0 365.8 %while.10 = (s32[]{:T(128)}, bf16[2,8,64,512]{3,2,1,0:T(8,128)(2,1)}, s32[2]{0:T(128)S(1)}, bf16[2,8,192,1024]{2,3,1,0:T(8,128)(2,1)}, pred[32]{0:T(512)(128)(4,...) while((s32[]{:T(128)}, ...), condition=%wide.region_4.5_spmd, body=%wide.region_1.4_spmd.sunk | while | flops 850403584 | bytes 223804016 | solution.py:158
  337.3 4.6 constant_dynamic-slice_fusion.11
  342.0 11.2 %reshape.186 = bf16[24,10,8,2,8,64]{5,4,3,2,1,0:T(8,128)(2,1)} reshape(bf16[24,80,1024]{2,1,0:T(8,128)(2,1)} %constant_dynamic-slice_fusion.11) | data formatting | bytes 7864320 | tf_op jit(solution)/shard_map/while/body/eval_jaxpr/reshape | solution.py:103
  353.2 5.6 fusion.127
  358.8 4.9 copy.160
  373.0 4.0 copy.161
  377.0 6.8 copy.162
  387.5 4.1 copy.163
  391.5 6.3 copy.164
  405.5 6.4 copy.166
  417.0 41.5 %fusion.131 = (f32[8,8,64]{2,1,0:T(8,128)S(1)}, f32[8,8,64,768]{3,2,1,0:T(8,128)}) fusion(pred[8,768]{1,0:T(8,128)(4,1)S(1)} %pad_add_fusion.5, f32[8]{0:T(128)S(1)} %get-tuple-element.209, f32[8,8,64,192]{3,2,1,0:T(8,128)S(1)} %fusion.126, f32[8,8,64,192]{3,2,1,0:T(8,128)} %copy.162, f32[8,8,64,192]{3,2,1,0:T(8,128)} %copy.164, ...), kind=kOutput, calls=%fused_computation.137.clone.1 | output fusion | flops 37749504 | bytes 25188384 | tf_op jit(solution)/shard_map/while/body/eval_jaxpr/sub | solution.py:138
  458.4 8.0 %divide_convert_fusion.2 = bf16[8,8,64,768]{3,2,1,0:T(8,128)(2,1)} fusion(f32[8,8,64,768]{3,2,1,0:T(8,128)} %get-tuple-element.165, f32[8,8,64]{2,1,0:T(8,128)S(1)} %get-tuple-element.166), kind=kLoop, calls=%fused_computation.3.clone.1 | loop fusion | flops 6291456 | bytes 18890752 | tf_op jit(solution)/shard_map/while/body/eval_jaxpr/convert_element_type | solution.py:139
  466.5 7.3 %fusion.132 = (bf16[8,8,64,192]{3,2,1,0:T(8,128)(2,1)}, bf16[8,8,64,192]{3,2,1,0:T(8,128)(2,1)}, bf16[8,8,64,192]{3,2,1,0:T(8,128)(2,1)}) fusion(bf16[8,8,64,768]{3,2,1,0:T(8,128)(2,1)} %divide_convert_fusion.2), kind=kLoop, calls=%fused_computation.136.clone.1 | loop fusion | bytes 9437184 | tf_op jit(solution)/shard_map/while/body/eval_jaxpr/slice | solution.py:147
  473.8 4.5 copy.169
  478.3 8.2 %fusion.135 = f32[8,8,64,64,1]{3,2,4,1,0:T(8,128)} fusion(bf16[8,8,64,24,8]{2,4,3,1,0:T(8,128)(2,1)} %bitcast.157, bf16[24,10,8,1,8,64]{5,4,3,2,1,0:T(8,128)(2,1)} %get-tuple-element.168), kind=kOutput, calls=%fused_computation.24.clone.1 | convolution fusion | flops 100663296 | bytes 4587520 | tf_op jit(solution)/shard_map/while/body/eval_jaxpr/chqrk,rckhd->cqhd/dot_general | solution.py:150
  486.5 4.7 copy.168
  491.2 8.2 %fusion.134 = f32[8,8,64,64,1]{3,2,4,1,0:T(8,128)} fusion(bf16[8,8,64,24,8]{2,4,3,1,0:T(8,128)(2,1)} %bitcast.159, bf16[24,10,8,1,8,64]{5,4,3,2,1,0:T(8,128)(2,1)} %get-tuple-element.168), kind=kOutput, calls=%fused_computation.22.clone.1 | convolution fusion | flops 100663296 | bytes 4587520 | tf_op jit(solution)/shard_map/while/body/eval_jaxpr/chqrk,rckhd->cqhd/dot_general | solution.py:150
  499.4 4.5 copy.167
  503.9 7.0 fusion.133
  518.4 4.6 constant_dynamic-slice_fusion.11
  523.0 11.2 %reshape.186 = bf16[24,10,8,2,8,64]{5,4,3,2,1,0:T(8,128)(2,1)} reshape(bf16[24,80,1024]{2,1,0:T(8,128)(2,1)} %constant_dynamic-slice_fusion.11) | data formatting | bytes 7864320 | tf_op jit(solution)/shard_map/while/body/eval_jaxpr/reshape | solution.py:103
  534.3 5.6 fusion.127
  539.9 4.9 copy.160
  554.1 4.0 copy.161
  558.1 6.5 copy.162
  568.2 4.1 copy.163
  572.3 6.3 copy.164
  586.2 6.4 copy.166
  597.7 41.5 %fusion.131 = (f32[8,8,64]{2,1,0:T(8,128)S(1)}, f32[8,8,64,768]{3,2,1,0:T(8,128)}) fusion(pred[8,768]{1,0:T(8,128)(4,1)S(1)} %pad_add_fusion.5, f32[8]{0:T(128)S(1)} %get-tuple-element.209, f32[8,8,64,192]{3,2,1,0:T(8,128)S(1)} %fusion.126, f32[8,8,64,192]{3,2,1,0:T(8,128)} %copy.162, f32[8,8,64,192]{3,2,1,0:T(8,128)} %copy.164, ...), kind=kOutput, calls=%fused_computation.137.clone.1 | output fusion | flops 37749504 | bytes 25188384 | tf_op jit(solution)/shard_map/while/body/eval_jaxpr/sub | solution.py:138
  639.2 8.0 %divide_convert_fusion.2 = bf16[8,8,64,768]{3,2,1,0:T(8,128)(2,1)} fusion(f32[8,8,64,768]{3,2,1,0:T(8,128)} %get-tuple-element.165, f32[8,8,64]{2,1,0:T(8,128)S(1)} %get-tuple-element.166), kind=kLoop, calls=%fused_computation.3.clone.1 | loop fusion | flops 6291456 | bytes 18890752 | tf_op jit(solution)/shard_map/while/body/eval_jaxpr/convert_element_type | solution.py:139
  647.3 7.3 %fusion.132 = (bf16[8,8,64,192]{3,2,1,0:T(8,128)(2,1)}, bf16[8,8,64,192]{3,2,1,0:T(8,128)(2,1)}, bf16[8,8,64,192]{3,2,1,0:T(8,128)(2,1)}) fusion(bf16[8,8,64,768]{3,2,1,0:T(8,128)(2,1)} %divide_convert_fusion.2), kind=kLoop, calls=%fused_computation.136.clone.1 | loop fusion | bytes 9437184 | tf_op jit(solution)/shard_map/while/body/eval_jaxpr/slice | solution.py:147
  654.6 4.5 copy.169
  659.1 8.2 %fusion.135 = f32[8,8,64,64,1]{3,2,4,1,0:T(8,128)} fusion(bf16[8,8,64,24,8]{2,4,3,1,0:T(8,128)(2,1)} %bitcast.157, bf16[24,10,8,1,8,64]{5,4,3,2,1,0:T(8,128)(2,1)} %get-tuple-element.168), kind=kOutput, calls=%fused_computation.24.clone.1 | convolution fusion | flops 100663296 | bytes 4587520 | tf_op jit(solution)/shard_map/while/body/eval_jaxpr/chqrk,rckhd->cqhd/dot_general | solution.py:150
  667.3 4.9 copy.168
  672.2 8.2 %fusion.134 = f32[8,8,64,64,1]{3,2,4,1,0:T(8,128)} fusion(bf16[8,8,64,24,8]{2,4,3,1,0:T(8,128)(2,1)} %bitcast.159, bf16[24,10,8,1,8,64]{5,4,3,2,1,0:T(8,128)(2,1)} %get-tuple-element.168), kind=kOutput, calls=%fused_computation.22.clone.1 | convolution fusion | flops 100663296 | bytes 4587520 | tf_op jit(solution)/shard_map/while/body/eval_jaxpr/chqrk,rckhd->cqhd/dot_general | solution.py:150
  680.4 4.5 copy.167
  684.9 7.0 fusion.133
  705.3 7.4 %fusion.43 = bf16[1024,512]{1,0:T(8,128)(2,1)} fusion(bf16[1024,512]{1,0:T(8,128)(2,1)S(1)} %get-tuple-element.101, bf16[2048,512]{1,0:T(8,128)(2,1)S(1)} %copy-done, bf16[512,2048]{1,0:T(8,128)(2,1)} %param.26, f32[512]{0:T(512)S(1)} %copy-done.13, f32[1024]{0:T(1024)S(1)} %add_rsqrt_fusion.1), kind=kOutput, calls=%fused_computation.67 | convolution fusion | flops 4317511680 | bytes 6297600 | tf_op jit(solution)/shard_map/dot_general | solution.py:173
  (122 shorter events, 89.1 us)
Async XLA Ops:
  0.0 705.3 %copy-start = (bf16[2048,512]{1,0:T(8,128)(2,1)S(1)}, bf16[2048,512]{1,0:T(8,128)(2,1)}, u32[]{:S(2)}) copy-start(bf16[2048,512]{1,0:T(8,128)(2,1)} %param.27) | copy-start | bytes 6291460
  0.0 5.2 copy-start.12
  5.1 20.9 %copy-start.7 = (bf16[16,64,512]{2,1,0:T(8,128)(2,1)}, bf16[16,64,512]{2,1,0:T(8,128)(2,1)S(1)}, u32[]{:S(2)}) copy-start(bf16[16,64,512]{2,1,0:T(8,128)(2,1)S(1)} %multiply_convert_fusion) | copy-start | bytes 3145732
  15.1 278.4 %all-to-all-start = ((bf16[128,64,1024]{2,1,0:T(8,128)(2,1)}), bf16[128,64,1024]{2,1,0:T(8,128)(2,1)}, u32[]{:S(2)}, u32[]{:S(2)}) async-start(bf16[128,64,1024]{2,1,0:T(8,128)(2,1)} %stack.2), calls=%async_computation | async-start | bytes 33554432 | tf_op jit(solution)/shard_map/all_to_all | solution.py:88
  28.5 1.3 copy-start.5
  29.8 4.7 copy-start.11
  31.3 127.5 %collective-permute-start = (bf16[8,64,1024]{2,1,0:T(8,128)(2,1)}, bf16[8,64,1024]{2,1,0:T(8,128)(2,1)S(1)}, u32[]{:S(2)}, u32[]{:S(2)}) collective-permute-start(bf16[8,64,1024]{2,1,0:T(8,128)(2,1)} %bitcast.39), channel_id=1, source_target_pairs={{0,16},{16,32},{32,48},{48,64},{64,80},{80,96},{96,112},{112,0},{1... | collective-permute-start | bytes 3145736 | tf_op jit(solution)/shard_map/ppermute | solution.py:20
  31.5 127.4 %collective-permute-start.1 = (bf16[8,64,1024]{2,1,0:T(8,128)(2,1)}, bf16[8,64,1024]{2,1,0:T(8,128)(2,1)}, u32[]{:S(2)}, u32[]{:S(2)}) collective-permute-start(bf16[8,64,1024]{2,1,0:T(8,128)(2,1)} %bitcast.41), channel_id=1, source_target_pairs={{16,0},{32,16},{48,32},{64,48},{80,64},{96,80},{112,96},{0,112},{1... | collective-permute-start | bytes 3145736 | tf_op jit(solution)/shard_map/ppermute | solution.py:21
  38.1 3.2 copy-start.14
  38.1 3.2 copy-start.10
  40.2 131.5 %copy-start.8 = (s32[2,8,192]{2,1,0:T(8,128)S(1)}, s32[2,8,192]{2,1,0:T(8,128)}, u32[]{:S(2)}) copy-start(s32[2,8,192]{2,1,0:T(8,128)} %copy.71) | copy-start | bytes 36868
  41.3 246.8 %copy-start.6 = (bf16[1024,1024]{1,0:T(8,128)(2,1)S(1)}, bf16[1024,1024]{1,0:T(8,128)(2,1)}, u32[]{:S(2)}) copy-start(bf16[1024,1024]{1,0:T(8,128)(2,1)} %copy-done.5) | copy-start | bytes 6291460
  160.1 95.5 %collective-permute-start.2 = (bf16[32,8,1024]{2,1,0:T(8,128)(2,1)S(1)}, bf16[32,8,1024]{2,1,0:T(8,128)(2,1)S(1)}, u32[]{:S(2)}, u32[]{:S(2)}) collective-permute-start(bf16[32,8,1024]{2,1,0:T(8,128)(2,1)S(1)} %get-tuple-element.96), channel_id=1, source_target_pairs={{0,1},{1,2},{2,3},{3,4},{4,5},{5,6},{6,7},{7,8},{8,9},{9,10},{10,1... | collective-permute-start | bytes 1572872 | tf_op jit(solution)/shard_map/ppermute | solution.py:20
  171.7 116.4 %collective-permute-start.3 = (bf16[32,8,1024]{2,1,0:T(8,128)(2,1)S(1)}, bf16[32,8,1024]{2,1,0:T(8,128)(2,1)S(1)}, u32[]{:S(2)}, u32[]{:S(2)}) collective-permute-start(bf16[32,8,1024]{2,1,0:T(8,128)(2,1)S(1)} %get-tuple-element.97), channel_id=1, source_target_pairs={{1,0},{2,1},{3,2},{4,3},{5,4},{6,5},{7,6},{8,7},{9,8},{10,9},{11,1... | collective-permute-start | bytes 1572872 | tf_op jit(solution)/shard_map/ppermute | solution.py:21
  328.4 7.6 %copy-start.9 = (s32[2,8,48]{2,1,0:T(8,128)S(1)}, s32[2,8,48]{2,1,0:T(8,128)}, u32[]{:S(2)}) copy-start(s32[2,8,48]{2,1,0:T(8,128)} %param.24) | copy-start | bytes 9220
  415.0 2.0 copy-start.1
  503.9 7.0 copy-start.2
  503.9 7.0 copy-start.3
  503.9 7.0 copy-start.4
  595.7 2.0 copy-start.1
  684.9 7.0 copy-start.2
  684.9 7.0 copy-start.3
  684.9 7.0 copy-start.4
  701.7 3.6 copy-start.13
